TPU v7x, 32 devices: a whole 2x2x4 slice. The times are simulated.
32 devices in a mesh: dp: 8 (over z, y), mp: 4 (over x, core).
Axes of the slice: x: 2, y: 2, z: 4, core: 2. Of those that a mesh axis runs over, the one named last changes fastest.
Arguments:
- tokens: bfloat16 [2, 4096, 768], P(None, 'dp'), may hold values from -6 to 6
- cotangent: bfloat16 [2, 4096, 768], P(None, 'dp'), may hold values from -6 to 6
- qkv_weight: bfloat16 [768, 3, 768], P('dp', None, 'mp'), may hold values from -0.21875 to 0.21875
- head_bias: bfloat16 [2, 4, 192], P(None, 'mp', 'dp'), may hold values from -3 to 3
- out_weight: bfloat16 [768, 768], P('mp', 'dp'), may hold values from -0.875 to 0.875
- up_weight: bfloat16 [768, 3072], P('dp', 'mp'), may hold values from -0.21875 to 0.21875
- up_bias: bfloat16 [4, 768], P('mp', 'dp'), may hold values from -3 to 3
- down_weight: bfloat16 [3072, 768], P('mp', 'dp'), may hold values from -0.109375 to 0.109375
- mem_qk: bfloat16 [2, 768, 768], P(None, 'dp'), may hold values from -0.21875 to 0.21875
- mem_value: bfloat16 [768, 768], P('dp'), may hold values from -0.875 to 0.875
- norm_gain: bfloat16 [2, 768], P(None, 'dp'), may hold values from 0.5 to 1.5
- shift_bias: bfloat16 [4, 768], P(None, 'dp'), may hold values from -2 to 2
- parents: int32 [2, 8], replicated, may hold values from -1 to 6, as said below
Outputs:
- mixed: bfloat16 [2, 4096, 768], P(None, ('dp', 'mp'))
- tokens_grad: bfloat16 [2, 4096, 768], P(None, 'dp')
- qkv_grad: float32 [768, 3, 768], P('dp', None, 'mp')
- head_bias_grad: float32 [2, 4, 192], P(None, 'mp', 'dp')
- out_grad: float32 [768, 768], P('mp', 'dp')
- up_grad: float32 [768, 3072], P('dp', 'mp')
- up_bias_grad: float32 [4, 768], P('mp', 'dp')
- down_grad: float32 [3072, 768], P('mp', 'dp')
- mem_qk_grad: float32 [2, 768, 768], P(None, 'dp')
- mem_value_grad: float32 [768, 768], P('dp')
- norm_gain_grad: float32 [2, 768], P(None, 'dp')
- shift_bias_grad: float32 [4, 768], P(None, 'dp')
Inputs may be any that keep to these rules, and one draw needn't show every extreme that they name: parents[b, n] is the parent segment of segment n in micro-batch b: -1 for the first segment of each aligned group of 8 segments, else an earlier segment of the same group; the last segment of each group has the segment before it as parent.
All inputs are finite; a program needn't handle non-finite values.
Results may differ from a plain program's by a relative error of at most 0.015.
Values may be sent and summed in bfloat16 or wider, within the bound.
A program may use at most 256 MiB of HBM per device.

v0:
```python
import jax
import jax.numpy as jnp
from jax import lax
from jax.sharding import PartitionSpec as P

HEAD_DIM = 64
MEM = 16
TREE = 8
MICRO = 2


EPSILON = 1e-05


def shifted(value, axis, steps):
    count = lax.axis_size(axis)
    initial, last = (max(0, -steps), min(count, count - steps))
    return lax.ppermute(value, axis, [(source, source + steps) for source in range(initial, last)])


def layer_norm(values, gains, offset):
    center = values - jnp.mean(values, -1, keepdims=True)
    spread = jnp.mean(center * center, -1, keepdims=True)
    return center * lax.rsqrt(spread + EPSILON) * gains + offset


def gelu_tanh(values):
    return jax.nn.gelu(values, approximate=True)


def rectify(values):
    return jnp.concatenate([jax.nn.relu(values), jax.nn.relu(-values)], -1)


def dpfp_rounded(values):
    rectified = rectify(values)
    return jnp.concatenate(
        [
            (rectified * jnp.roll(rectified, roll_by, -1)).astype(jnp.bfloat16)
            for roll_by in (1, 2, 3)
        ],
        -1,
    )


def dpfp_backward(values, grad_feats):
    rectified = rectify(values)
    width = rectified.shape[1]
    grad_rect = jnp.zeros_like(rectified)
    for place, roll_by in enumerate((1, 2, 3)):
        piece = grad_feats[:, place * width : (place + 1) * width]
        grad_rect = (
            grad_rect
            + piece * jnp.roll(rectified, roll_by, -1)
            + jnp.roll(piece * rectified, -roll_by, -1)
        )
    half = width // 2
    positive = (values > 0).astype(jnp.float32)
    negative = (values < 0).astype(jnp.float32)
    return grad_rect[:, :half] * positive - grad_rect[:, half:] * negative


def divide_rows(top_part, bottom_part):
    return top_part / bottom_part


def inner_rows(left, right):
    return lax.dot_general(
        left, right, (((0,), (0,)), ((), ())), preferred_element_type=jnp.float32
    )


def outer_cols(left, right):
    return lax.dot_general(
        left, right, (((1,), (1,)), ((), ())), preferred_element_type=jnp.float32
    )


def path_marks(parent_row, own_index):
    seg_count = parent_row.shape[0]
    places = jnp.arange(seg_count, dtype=jnp.int32)

    def parent_of(position):
        return jnp.sum(jnp.where(places == position, parent_row, 0))

    current = parent_of(own_index)
    base_index = own_index // TREE * TREE
    members = base_index + jnp.arange(TREE, dtype=jnp.int32)
    ancestors = jnp.zeros((TREE,), jnp.float32)
    for hop_index in range(TREE - 1):
        ancestors = ancestors + (members == current).astype(jnp.float32)
        current = jnp.where(current >= 0, parent_of(current), -1)
    return ancestors


def body(
    tokens,
    cotangent,
    qkv_weight,
    head_bias,
    out_weight,
    up_weight,
    up_bias,
    down_weight,
    mem_qk,
    mem_value,
    norm_gain,
    shift_bias,
    parents,
):
    own_index = lax.axis_index("dp")
    own_slot = own_index % TREE
    seg_len = tokens.shape[1]
    model_width = mem_value.shape[1]
    local_cols = qkv_weight.shape[2]
    heads_local = local_cols // HEAD_DIM
    group_rows = TREE * MEM
    score_scale = HEAD_DIM ** (-0.5)
    share_rows = seg_len // lax.axis_size("mp")
    share_start = lax.axis_index("mp") * share_rows
    rows_index = jnp.arange(seg_len)
    causal = rows_index[:, None] >= rows_index[None, :]
    totals = None
    outputs = []
    input_grads = []
    for micro_index in range(MICRO):
        gathered = (
            lax.all_gather(qkv_weight, "dp", axis=0, tiled=True),
            lax.all_gather(head_bias, "dp", axis=2, tiled=True),
            lax.all_gather(out_weight, "dp", axis=1, tiled=True),
            lax.all_gather(up_weight, "dp", axis=0, tiled=True),
            lax.all_gather(up_bias, "dp", axis=1, tiled=True),
            lax.all_gather(down_weight, "dp", axis=1, tiled=True),
            lax.all_gather(mem_qk, "dp", axis=1, tiled=True),
            lax.all_gather(mem_value, "dp", axis=0, tiled=True),
            lax.all_gather(norm_gain, "dp", axis=1, tiled=True),
            lax.all_gather(shift_bias, "dp", axis=1, tiled=True),
        )
        (
            qkv_full,
            hbias_full,
            outw_full,
            upw_full,
            ubias_full,
            downw_full,
            memqk_full,
            memv_full,
            gains_full,
            shifts_full,
        ) = gathered
        inputs = tokens[micro_index]
        memory_rows = inputs[seg_len - MEM :]
        key_raw = jnp.dot(memory_rows, memqk_full[1], preferred_element_type=jnp.float32)
        value_raw = jnp.dot(memory_rows, memv_full, preferred_element_type=jnp.float32)
        key_low = key_raw.astype(jnp.bfloat16)
        value_low = value_raw.astype(jnp.bfloat16)
        empty_group = jnp.zeros((group_rows, model_width), jnp.bfloat16)
        group_keys = lax.dynamic_update_slice_in_dim(empty_group, key_low, own_slot * MEM, 0)
        group_values = lax.dynamic_update_slice_in_dim(empty_group, value_low, own_slot * MEM, 0)
        for hop_count in range(1, TREE):
            far_keys, far_values = shifted((key_low, value_low), "dp", hop_count)
            far_slot = own_slot - hop_count
            inside = far_slot >= 0
            place_at = jnp.maximum(far_slot, 0) * MEM
            group_keys = jnp.where(
                inside,
                lax.dynamic_update_slice_in_dim(group_keys, far_keys, place_at, 0),
                group_keys,
            )
            group_values = jnp.where(
                inside,
                lax.dynamic_update_slice_in_dim(group_values, far_values, place_at, 0),
                group_values,
            )
        group_keys_f = group_keys.astype(jnp.float32)
        key_feats = dpfp_rounded(group_keys_f)
        row_mask = jnp.repeat(path_marks(parents[micro_index], own_index), MEM)
        query_raw = jnp.dot(inputs, memqk_full[0], preferred_element_type=jnp.float32)
        query_feats = dpfp_rounded(query_raw)
        masked_scores = outer_cols(query_feats, key_feats) * row_mask[None, :]
        read_weights = masked_scores.astype(jnp.bfloat16)
        denominator = jnp.sum(masked_scores, -1, keepdims=True) + 1.0
        numerator = jnp.dot(read_weights, group_values, preferred_element_type=jnp.float32)
        hidden = inputs.astype(jnp.float32) + numerator / denominator
        attn_in = layer_norm(hidden, gains_full[0], shifts_full[0]).astype(jnp.bfloat16)
        projected = jnp.einsum("sd,dcf->scf", attn_in, qkv_full, preferred_element_type=jnp.float32)
        bias_pair = hbias_full.reshape(2, local_cols).astype(jnp.float32)
        shape_heads = (seg_len, heads_local, HEAD_DIM)
        queries = (projected[:, 0] + bias_pair[0]).astype(jnp.bfloat16).reshape(shape_heads)
        key_heads = projected[:, 1].astype(jnp.bfloat16).reshape(shape_heads)
        value_heads = (projected[:, 2] + bias_pair[1]).astype(jnp.bfloat16).reshape(shape_heads)
        scores = (
            jnp.einsum("qhd,khd->hqk", queries, key_heads, preferred_element_type=jnp.float32)
            * score_scale
        )
        scores = jnp.where(causal[None], scores, -jnp.inf)
        row_max = jnp.max(scores, -1, keepdims=True)
        exponents = jnp.exp(scores - row_max)
        row_total = jnp.sum(exponents, -1, keepdims=True)
        log_total = row_max + jnp.log(row_total)
        prob_low = (exponents / row_total).astype(jnp.bfloat16)
        attended = jnp.einsum(
            "hqk,khd->qhd", prob_low, value_heads, preferred_element_type=jnp.float32
        )
        attended = attended.astype(jnp.bfloat16).reshape(seg_len, local_cols)
        attn_out = (
            lax.psum(
                jnp.dot(attended, outw_full, preferred_element_type=jnp.float32).astype(
                    jnp.bfloat16
                ),
                "mp",
            ).astype(jnp.float32)
            + shifts_full[2]
        )
        middle = hidden + attn_out
        normed_two = layer_norm(middle, gains_full[1], shifts_full[1]).astype(jnp.bfloat16)
        pre_act = jnp.dot(normed_two, upw_full, preferred_element_type=jnp.float32) + ubias_full[0]
        activated = gelu_tanh(pre_act).astype(jnp.bfloat16)
        mlp_share = lax.psum_scatter(
            jnp.dot(activated, downw_full, preferred_element_type=jnp.float32).astype(jnp.bfloat16),
            "mp",
            scatter_dimension=0,
            tiled=True,
        ).astype(jnp.float32)
        middle_share = lax.dynamic_slice_in_dim(middle, share_start, share_rows, 0)
        outputs.append((middle_share + mlp_share + shifts_full[3]).astype(jnp.bfloat16))
        weights_again = (
            lax.all_gather(qkv_weight, "dp", axis=0, tiled=True),
            lax.all_gather(head_bias, "dp", axis=2, tiled=True),
            lax.all_gather(out_weight, "dp", axis=1, tiled=True),
            lax.all_gather(up_weight, "dp", axis=0, tiled=True),
            lax.all_gather(up_bias, "dp", axis=1, tiled=True),
            lax.all_gather(down_weight, "dp", axis=1, tiled=True),
            lax.all_gather(mem_qk, "dp", axis=1, tiled=True),
            lax.all_gather(mem_value, "dp", axis=0, tiled=True),
            lax.all_gather(norm_gain, "dp", axis=1, tiled=True),
            lax.all_gather(shift_bias, "dp", axis=1, tiled=True),
        )
        qkv_back = weights_again[0]
        outw_back = weights_again[2]
        upw_back = weights_again[3]
        downw_back = weights_again[5]
        memqk_back = weights_again[6]
        memv_back = weights_again[7]
        gains_back = weights_again[8]
        shifts_back = weights_again[9]
        grad_out = cotangent[micro_index]
        grad_out_f = grad_out.astype(jnp.float32)
        grad_downw = inner_rows(activated, grad_out)
        grad_act = outer_cols(grad_out, downw_back)
        gelu_value, gelu_back = jax.vjp(gelu_tanh, pre_act)
        grad_pre = gelu_back(grad_act)[0].astype(jnp.bfloat16)
        grad_ubias = jnp.sum(grad_pre.astype(jnp.float32), 0)[None, :]
        grad_upw = inner_rows(normed_two, grad_pre)
        grad_norm_two = lax.psum(outer_cols(grad_pre, upw_back).astype(jnp.bfloat16), "mp").astype(
            jnp.float32
        )
        norm_value, norm_two_back = jax.vjp(layer_norm, middle, gains_back[1], shifts_back[1])
        grad_mid_norm, gain_two, shift_two = norm_two_back(grad_norm_two)
        grad_middle = grad_out_f + grad_mid_norm
        grad_attn = grad_middle.astype(jnp.bfloat16)
        grad_outw = inner_rows(attended, grad_attn)
        grad_attended = outer_cols(grad_attn, outw_back).astype(jnp.bfloat16).reshape(shape_heads)
        scores_again = (
            jnp.einsum("qhd,khd->hqk", queries, key_heads, preferred_element_type=jnp.float32)
            * score_scale
        )
        scores_again = jnp.where(causal[None], scores_again, -jnp.inf)
        prob_full = jnp.exp(scores_again - log_total)
        prob_again = prob_full.astype(jnp.bfloat16)
        grad_values = jnp.einsum(
            "hqk,qhd->khd", prob_again, grad_attended, preferred_element_type=jnp.float32
        )
        grad_probs = jnp.einsum(
            "qhd,khd->hqk", grad_attended, value_heads, preferred_element_type=jnp.float32
        )
        row_delta = jnp.sum(prob_full * grad_probs, -1, keepdims=True)
        grad_scores = (prob_full * (grad_probs - row_delta)).astype(jnp.bfloat16)
        grad_queries = (
            jnp.einsum("hqk,khd->qhd", grad_scores, key_heads, preferred_element_type=jnp.float32)
            * score_scale
        )
        grad_keys = (
            jnp.einsum("hqk,qhd->khd", grad_scores, queries, preferred_element_type=jnp.float32)
            * score_scale
        )
        grad_proj = (
            jnp.stack([grad_queries, grad_keys, grad_values], 1)
            .reshape(seg_len, 3, local_cols)
            .astype(jnp.bfloat16)
        )
        grad_proj_f = grad_proj.astype(jnp.float32)
        grad_hbias = jnp.stack(
            [jnp.sum(grad_proj_f[:, 0], 0), jnp.sum(grad_proj_f[:, 2], 0)]
        ).reshape(2, 1, local_cols)
        grad_qkv = jnp.einsum("sd,scf->dcf", attn_in, grad_proj, preferred_element_type=jnp.float32)
        grad_norm_one = lax.psum(
            jnp.einsum(
                "scf,dcf->sd", grad_proj, qkv_back, preferred_element_type=jnp.float32
            ).astype(jnp.bfloat16),
            "mp",
        ).astype(jnp.float32)
        norm_value_one, norm_one_back = jax.vjp(layer_norm, hidden, gains_back[0], shifts_back[0])
        grad_hid_norm, gain_one, shift_one = norm_one_back(grad_norm_one)
        grad_hidden = grad_middle + grad_hid_norm
        ratio_value, divide_back = jax.vjp(divide_rows, numerator, denominator)
        grad_numerator, grad_denominator = divide_back(grad_hidden)
        grad_numerator_b = grad_numerator.astype(jnp.bfloat16)
        grad_read = outer_cols(grad_numerator_b, group_values)
        grad_values_group = inner_rows(read_weights, grad_numerator_b)
        grad_assoc = ((grad_read + grad_denominator) * row_mask[None, :]).astype(jnp.bfloat16)
        grad_query_feats = jnp.dot(grad_assoc, key_feats, preferred_element_type=jnp.float32)
        grad_key_feats = inner_rows(grad_assoc, query_feats)
        grad_query = dpfp_backward(query_raw, grad_query_feats).astype(jnp.bfloat16)
        grad_keys_group = dpfp_backward(group_keys_f, grad_key_feats)
        own_keys = lax.dynamic_slice_in_dim(grad_keys_group, own_slot * MEM, MEM, 0)
        own_values = lax.dynamic_slice_in_dim(grad_values_group, own_slot * MEM, MEM, 0)
        for hop_count in range(1, TREE):
            far_slot = own_slot - hop_count
            inside = far_slot >= 0
            take_at = jnp.maximum(far_slot, 0) * MEM
            send_keys = jnp.where(
                inside, lax.dynamic_slice_in_dim(grad_keys_group, take_at, MEM, 0), 0.0
            )
            send_values = jnp.where(
                inside, lax.dynamic_slice_in_dim(grad_values_group, take_at, MEM, 0), 0.0
            )
            back_keys, back_values = (
                shifted(send_keys.astype(jnp.bfloat16), "dp", -hop_count).astype(send_keys.dtype),
                shifted(send_values.astype(jnp.bfloat16), "dp", -hop_count).astype(
                    send_values.dtype
                ),
            )
            arrive = own_slot + hop_count < TREE
            own_keys = own_keys + jnp.where(arrive, back_keys, 0.0)
            own_values = own_values + jnp.where(arrive, back_values, 0.0)
        own_keys_b = own_keys.astype(jnp.bfloat16)
        own_values_b = own_values.astype(jnp.bfloat16)
        grad_memqk = jnp.stack(
            [inner_rows(inputs, grad_query), inner_rows(memory_rows, own_keys_b)]
        )
        grad_memv = inner_rows(memory_rows, own_values_b)
        memory_part = outer_cols(own_keys_b, memqk_back[1]) + outer_cols(own_values_b, memv_back)
        padding = jnp.zeros((seg_len - MEM, model_width), jnp.float32)
        grad_inputs = (
            grad_hidden
            + outer_cols(grad_query, memqk_back[0])
            + jnp.concatenate([padding, memory_part], 0)
        )
        input_grads.append(grad_inputs.astype(jnp.bfloat16))
        grad_gains = jnp.stack([gain_one, gain_two])
        grad_shifts = jnp.stack(
            [shift_one, shift_two, jnp.sum(grad_middle, 0), jnp.sum(grad_out_f, 0)]
        )
        shares = (
            grad_qkv,
            grad_hbias,
            grad_outw,
            grad_upw,
            grad_ubias,
            grad_downw,
            grad_memqk,
            grad_memv,
            grad_gains,
            grad_shifts,
        )
        totals = (
            shares
            if totals is None
            else tuple((older + newer for older, newer in zip(totals, shares)))
        )
    (
        sum_qkv,
        sum_hbias,
        sum_outw,
        sum_upw,
        sum_ubias,
        sum_downw,
        sum_memqk,
        sum_memv,
        sum_gains,
        sum_shifts,
    ) = totals
    totals = (
        lax.psum_scatter(sum_qkv, "dp", scatter_dimension=0, tiled=True),
        lax.psum_scatter(sum_hbias, "dp", scatter_dimension=2, tiled=True),
        lax.psum_scatter(sum_outw, "dp", scatter_dimension=1, tiled=True),
        lax.psum_scatter(sum_upw, "dp", scatter_dimension=0, tiled=True),
        lax.psum_scatter(sum_ubias, "dp", scatter_dimension=1, tiled=True),
        lax.psum_scatter(sum_downw, "dp", scatter_dimension=1, tiled=True),
        lax.psum_scatter(sum_memqk, "dp", scatter_dimension=1, tiled=True),
        lax.psum_scatter(sum_memv, "dp", scatter_dimension=0, tiled=True),
        lax.psum_scatter(sum_gains.astype(jnp.float32), "dp", scatter_dimension=1, tiled=True),
        lax.psum_scatter(sum_shifts, "dp", scatter_dimension=1, tiled=True),
    )
    mixed = jnp.stack(outputs)
    tokens_grad = jnp.stack(input_grads)
    return (mixed, tokens_grad) + tuple(totals)


def solution(mesh):
    return jax.shard_map(
        body,
        mesh=mesh,
        in_specs=(
            P(None, "dp", None),
            P(None, "dp", None),
            P("dp", None, "mp"),
            P(None, "mp", "dp"),
            P("mp", "dp"),
            P("dp", "mp"),
            P("mp", "dp"),
            P("mp", "dp"),
            P(None, "dp", None),
            P("dp", None),
            P(None, "dp"),
            P(None, "dp"),
            P(),
        ),
        out_specs=(
            P(None, ("dp", "mp"), None),
            P(None, "dp", None),
            P("dp", None, "mp"),
            P(None, "mp", "dp"),
            P("mp", "dp"),
            P("dp", "mp"),
            P("mp", "dp"),
            P("mp", "dp"),
            P(None, "dp", None),
            P("dp", None),
            P(None, "dp"),
            P(None, "dp"),
        ),
        check_vma=False,
    )
```

profile of v0, /device:TPU:0, one launch (start us, length us, event | category | flops | bytes accessed | tf_op | source)
XLA Modules:
  0.0 1381.0 jit_solution(7074386980268696026)
XLA Ops:
  31.6 22.7 %all-gather = bf16[8,96,2]{1,2,0:T(2,128)(2,1)S(1)} all-gather(bf16[1,96,2]{1,2,0:T(2,128)(2,1)} %bitcast.335), channel_id=1, replica_groups=mesh['dp'=8,'mp'=4] {'dp'}, dimensions={0}, use_global_device_ids=true | all-gather | bytes 3456 | tf_op jit(solution)/shard_map/all_gather | solution.py:136
  54.4 17.0 %all-gather.1 = bf16[8,96,4]{1,2,0:T(4,128)(2,1)S(1)} all-gather(bf16[1,96,4]{1,2,0:T(4,128)(2,1)} %bitcast.334), channel_id=1, replica_groups=mesh['dp'=8,'mp'=4] {'dp'}, dimensions={0}, use_global_device_ids=true | all-gather | bytes 6912 | tf_op jit(solution)/shard_map/all_gather | solution.py:137
  73.1 31.3 %all_gather.25 = bf16[2,1,192]{1,0,2:T(2,128)(2,1)S(1)} all-gather(bf16[2,1,24]{1,0,2:T(2,128)(2,1)S(1)} %copy.89), channel_id=1, replica_groups=mesh['dp'=8,'mp'=4] {'dp'}, dimensions={2}, use_global_device_ids=true | all-gather | bytes 864 | tf_op jit(solution)/shard_map/all_gather | solution.py:129
  107.1 34.7 %all_gather.24 = bf16[768,3,192]{2,1,0:T(4,128)(2,1)S(1)} all-gather(bf16[96,3,192]{2,1,0:T(4,128)(2,1)S(1)} %copy.87), channel_id=1, replica_groups=mesh['dp'=8,'mp'=4] {'dp'}, dimensions={0}, use_global_device_ids=true | all-gather | bytes 995328 | tf_op jit(solution)/shard_map/all_gather | solution.py:128
  145.3 33.0 %all_gather.26 = bf16[192,768]{0,1:T(8,128)(2,1)} all-gather(bf16[192,96]{0,1:T(8,128)(2,1)S(1)} %copy.91), channel_id=1, replica_groups=mesh['dp'=8,'mp'=4] {'dp'}, dimensions={1}, use_global_device_ids=true | all-gather | bytes 331776 | tf_op jit(solution)/shard_map/all_gather | solution.py:130
  218.9 6.6 collective-permute-start.12
  349.6 22.7 %all-reduce.2 = bf16[768]{0:T(1024)(128)(2,1)S(1)} all-reduce(bf16[768]{0:T(1024)(128)(2,1)} %dynamic-update-slice.28), channel_id=1, replica_groups=mesh['dp'=8,'mp'=4] {'dp'}, use_global_device_ids=true, to_apply=%add.2 | all-reduce | flops 768 | bytes 3072
  372.9 17.3 %all-reduce.19.cloned.1.call-done = (bf16[512,768]{1,0:T(8,128)(2,1)}, bf16[512,768]{1,0:T(8,128)(2,1)}) async-done(((bf16[512,768]{1,0:T(8,128)(2,1)}, bf16[512,768]{1,0:T(8,128)(2,1)}), (bf16[512,768]{1,0:T(8,128)(2,1)}, bf16[512,768]{1,0:T(8,128)(2,1)})) %all-reduce.19.cloned.1.call-update) | async-done | bytes 1572880 | tf_op jit(solution)/shard_map/psum | solution.py:207
  395.8 37.6 %all-gather.11.cloned.1.call-done = bf16[768,768]{1,0:T(8,128)(2,1)} async-done(((bf16[96,768]{1,0:T(8,128)(2,1)}), bf16[768,768]{1,0:T(8,128)(2,1)}) %all-gather.11.cloned.1.call-update) | async-done | bytes 1179664 | tf_op jit(solution)/shard_map/all_gather | solution.py:131
  437.3 38.0 %all-gather.13.cloned.1.call-done = bf16[768,768]{0,1:T(8,128)(2,1)} async-done(((bf16[768,96]{0,1:T(8,128)(2,1)}), bf16[768,768]{0,1:T(8,128)(2,1)}) %all-gather.13.cloned.1.call-update) | async-done | bytes 1179664 | tf_op jit(solution)/shard_map/all_gather | solution.py:133
  491.0 39.4 %all-reduce.17.cloned.1.call-done = (bf16[512,768]{1,0:T(8,128)(2,1)}, bf16[512,768]{1,0:T(8,128)(2,1)}) async-done(((bf16[512,768]{1,0:T(8,128)(2,1)}, bf16[512,768]{1,0:T(8,128)(2,1)}), (bf16[512,768]{1,0:T(8,128)(2,1)}, bf16[512,768]{1,0:T(8,128)(2,1)})) %all-reduce.17.cloned.1.call-update) | async-done | bytes 1572880 | tf_op jit(solution)/shard_map/psum | solution.py:255
  577.9 21.1 %all-reduce.15.cloned.1.call-done = (bf16[512,768]{1,0:T(8,128)(2,1)}, bf16[512,768]{1,0:T(8,128)(2,1)}) async-done(((bf16[512,768]{1,0:T(8,128)(2,1)}, bf16[512,768]{1,0:T(8,128)(2,1)}), (bf16[512,768]{1,0:T(8,128)(2,1)}, bf16[512,768]{1,0:T(8,128)(2,1)})) %all-reduce.15.cloned.1.call-update) | async-done | bytes 1572880 | tf_op jit(solution)/shard_map/psum | solution.py:297
  647.1 6.1 slice_multiply_fusion
  671.2 9.1 slice_multiply_fusion.3
  707.7 9.4 fusion.13
  724.4 7.1 fusion.9
  760.2 8.2 copy.106
  830.3 17.9 %all-reduce.3 = f32[2,1,192]{2,1,0:T(1,128)S(1)} all-reduce(f32[2,1,192]{2,1,0:T(1,128)S(1)} %maximum_add_fusion.7), channel_id=5, replica_groups=mesh['dp'=8,'mp'=4] {'dp'}, use_global_device_ids=true, to_apply=%region_53.54.clone | all-reduce | flops 384 | bytes 3072
  862.6 48.0 %reduce-scatter.32.cloned.1.call-done = f32[96,192]{1,0:T(8,128)} async-done(((f32[768,192]{1,0:T(8,128)}), f32[96,192]{1,0:T(8,128)}) %reduce-scatter.32.cloned.1.call-update) | async-done | bytes 73744
  912.3 170.4 %all-reduce.13.cloned.1.call-done = f32[2,768,768]{2,0,1:T(2,128)} async-done(((f32[2,768,768]{2,0,1:T(2,128)}), f32[2,768,768]{2,0,1:T(2,128)}) %all-reduce.13.cloned.1.call-update) | async-done | bytes 4718608
  1084.6 70.6 %reduce-scatter.26.cloned.1.call-done = f32[96,3,192]{2,0,1:T(8,128)} async-done(((f32[768,3,192]{2,0,1:T(8,128)}), f32[96,3,192]{2,0,1:T(8,128)}) %reduce-scatter.26.cloned.1.call-update) | async-done | bytes 221200 | tf_op jit(solution)/shard_map/reduce_scatter | solution.py:385
  1155.2 72.8 %reduce-scatter.30.cloned.1.call-done = f32[768,96]{0,1:T(8,128)} async-done(((f32[768,768]{0,1:T(8,128)}), f32[768,96]{0,1:T(8,128)}) %reduce-scatter.30.cloned.1.call-update) | async-done | bytes 294928 | tf_op jit(solution)/shard_map/reduce_scatter | solution.py:390
  1228.0 72.8 %reduce-scatter.28.cloned.1.call-done = f32[96,768]{1,0:T(8,128)} async-done(((f32[768,768]{1,0:T(8,128)}), f32[96,768]{1,0:T(8,128)}) %reduce-scatter.28.cloned.1.call-update) | async-done | bytes 294928 | tf_op jit(solution)/shard_map/reduce_scatter | solution.py:388
  1300.8 72.9 %reduce-scatter.36.cloned.1.call-done = f32[96,768]{1,0:T(8,128)} async-done(((f32[768,768]{1,0:T(8,128)}), f32[96,768]{1,0:T(8,128)}) %reduce-scatter.36.cloned.1.call-update) | async-done | bytes 294928
  (926 shorter events, 464.7 us)
Async XLA Ops:
  7.2 171.0 %all-gather.9.cloned.1.call-start = ((), (), s32[]{:S(2)}) async-start(), calls=%async_computation.11 | async-start | bytes 1327104 | tf_op jit(solution)/shard_map/all_gather | solution.py:135
  7.9 236.7 %all-gather.7.cloned.1.call-start = ((), (), s32[]{:S(2)}) async-start(), calls=%async_computation.10 | async-start | bytes 2654208 | tf_op jit(solution)/shard_map/all_gather | solution.py:134
  8.7 381.5 %all-reduce.19.cloned.1.call-start = ((), (), s32[]{:S(2)}) async-start(), calls=%async_computation.27 | async-start | bytes 3145728 | tf_op jit(solution)/shard_map/psum | solution.py:207
  181.1 58.1 %collective-permute-start.26 = (bf16[16,768]{1,0:T(8,128)(2,1)S(1)}, bf16[16,768]{1,0:T(8,128)(2,1)S(1)}, u32[]{:S(2)}, u32[]{:S(2)}) collective-permute-start(bf16[16,768]{1,0:T(8,128)(2,1)S(1)} %get-tuple-element.212), channel_id=1, source_target_pairs={{0,24},{4,28},{1,25},{5,29},{2,26},{6,30},{3,27},{7,31}} | collective-permute-start | bytes 73736 | tf_op jit(solution)/shard_map/ppermute | solution.py:18
  183.6 51.7 %collective-permute-start.25 = (bf16[16,768]{1,0:T(8,128)(2,1)S(1)}, bf16[16,768]{1,0:T(8,128)(2,1)S(1)}, u32[]{:S(2)}, u32[]{:S(2)}) collective-permute-start(bf16[16,768]{1,0:T(8,128)(2,1)S(1)} %get-tuple-element.212), channel_id=1, source_target_pairs={{0,20},{4,24},{8,28},{1,21},{5,25},{9,29},{2,22},{6,26},{10,30},{3... | collective-permute-start | bytes 73736 | tf_op jit(solution)/shard_map/ppermute | solution.py:18
  184.9 42.0 %collective-permute-start.24 = (bf16[16,768]{1,0:T(8,128)(2,1)S(1)}, bf16[16,768]{1,0:T(8,128)(2,1)S(1)}, u32[]{:S(2)}, u32[]{:S(2)}) collective-permute-start(bf16[16,768]{1,0:T(8,128)(2,1)S(1)} %get-tuple-element.212), channel_id=1, source_target_pairs={{0,16},{4,20},{8,24},{12,28},{1,17},{5,21},{9,25},{13,29},{2,18},{... | collective-permute-start | bytes 73736 | tf_op jit(solution)/shard_map/ppermute | solution.py:18
  246.2 42.6 %collective-permute-start.5 = (bf16[16,768]{1,0:T(8,128)(2,1)S(1)}, bf16[16,768]{1,0:T(8,128)(2,1)S(1)}, u32[]{:S(2)}, u32[]{:S(2)}) collective-permute-start(bf16[16,768]{1,0:T(8,128)(2,1)S(1)} %get-tuple-element.208), channel_id=1, source_target_pairs={{0,24},{4,28},{1,25},{5,29},{2,26},{6,30},{3,27},{7,31}} | collective-permute-start | bytes 73736 | tf_op jit(solution)/shard_map/ppermute | solution.py:18
  251.5 36.0 %collective-permute-start.4 = (bf16[16,768]{1,0:T(8,128)(2,1)S(1)}, bf16[16,768]{1,0:T(8,128)(2,1)S(1)}, u32[]{:S(2)}, u32[]{:S(2)}) collective-permute-start(bf16[16,768]{1,0:T(8,128)(2,1)S(1)} %get-tuple-element.208), channel_id=1, source_target_pairs={{0,20},{4,24},{8,28},{1,21},{5,25},{9,29},{2,22},{6,26},{10,30},{3... | collective-permute-start | bytes 73736 | tf_op jit(solution)/shard_map/ppermute | solution.py:18
  345.2 88.2 %all-gather.11.cloned.1.call-start = ((), (), s32[]{:S(2)}) async-start(), calls=%async_computation.12 | async-start | bytes 1327104 | tf_op jit(solution)/shard_map/all_gather | solution.py:131
  345.8 129.5 %all-gather.13.cloned.1.call-start = ((), (), s32[]{:S(2)}) async-start(), calls=%async_computation.13 | async-start | bytes 1327104 | tf_op jit(solution)/shard_map/all_gather | solution.py:133
  346.4 184.1 %all-reduce.17.cloned.1.call-start = ((), (), s32[]{:S(2)}) async-start(), calls=%async_computation.26 | async-start | bytes 3145728 | tf_op jit(solution)/shard_map/psum | solution.py:255
  488.7 110.2 %all-reduce.15.cloned.1.call-start = ((), (), s32[]{:S(2)}) async-start(), calls=%async_computation.25 | async-start | bytes 3145728 | tf_op jit(solution)/shard_map/psum | solution.py:297
  555.9 271.4 %reduce-scatter.34.cloned.1.call-start = ((), (), s32[]{:S(2)}) async-start(), calls=%async_computation.20 | async-start | bytes 442368
  557.5 291.4 %reduce-scatter.22.cloned.1.call-start = ((), (), s32[]{:S(2)}) async-start(), calls=%async_computation.14 | async-start | bytes 983040 | tf_op jit(solution)/shard_map/reduce_scatter | solution.py:219
  561.1 287.8 %reduce-scatter.24.cloned.1.call-start = ((), (), s32[]{:S(2)}) async-start(), calls=%async_computation.15 | async-start | bytes 983040 | tf_op jit(solution)/shard_map/reduce_scatter | solution.py:219
  565.0 285.9 %reduce-scatter.38.cloned.1.call-start = ((), (), s32[]{:S(2)}) async-start(), calls=%async_computation.22 | async-start | bytes 442368
  611.4 241.0 %reduce-scatter.40.cloned.1.call-start = ((), (), s32[]{:S(2)}) async-start(), calls=%async_computation.23 | async-start | bytes 442368
  614.4 296.2 %reduce-scatter.32.cloned.1.call-start = ((), (), s32[]{:S(2)}) async-start(), calls=%async_computation.19 | async-start | bytes 884736
  619.5 463.1 %all-reduce.13.cloned.1.call-start = ((), (), s32[]{:S(2)}) async-start(), calls=%async_computation.24 | async-start | bytes 9437184
  700.8 33.6 %collective-permute-start.28 = (bf16[16,768]{1,0:T(8,128)(2,1)}, bf16[16,768]{1,0:T(8,128)(2,1)S(1)}, u32[]{:S(2)}, u32[]{:S(2)}) collective-permute-start(bf16[16,768]{1,0:T(8,128)(2,1)} %get-tuple-element.160), channel_id=1, source_target_pairs={{4,0},{8,4},{12,8},{16,12},{20,16},{24,20},{28,24},{5,1},{9,5},{13... | collective-permute-start | bytes 73736 | tf_op jit(solution)/shard_map/ppermute | solution.py:18
  768.5 386.7 %reduce-scatter.26.cloned.1.call-start = ((), (), s32[]{:S(2)}) async-start(), calls=%async_computation.16 | async-start | bytes 2654208 | tf_op jit(solution)/shard_map/reduce_scatter | solution.py:385
  775.2 452.8 %reduce-scatter.30.cloned.1.call-start = ((), (), s32[]{:S(2)}) async-start(), calls=%async_computation.18 | async-start | bytes 2654208 | tf_op jit(solution)/shard_map/reduce_scatter | solution.py:390
  781.6 519.2 %reduce-scatter.28.cloned.1.call-start = ((), (), s32[]{:S(2)}) async-start(), calls=%async_computation.17 | async-start | bytes 2654208 | tf_op jit(solution)/shard_map/reduce_scatter | solution.py:388
  787.8 585.9 %reduce-scatter.36.cloned.1.call-start = ((), (), s32[]{:S(2)}) async-start(), calls=%async_computation.21 | async-start | bytes 2654208
  (294 other events, 2065.7 us)
Sparse Core Ops, SparseCore 0:
  10.2 43.8 all-gather.8
  56.2 57.5 all-gather.6
  345.3 44.8 all-reduce.18
  392.2 41.1 all-gather.10
  435.5 39.7 all-gather.12
  488.9 41.5 all-reduce.16
  556.0 42.9 all-reduce.14
  602.2 62.3 reduce-scatter.33
  667.1 22.2 reduce-scatter.21
  691.8 23.1 reduce-scatter.23
  718.3 62.2 reduce-scatter.37
  783.7 61.2 reduce-scatter.39
  848.3 62.2 reduce-scatter.31
  914.1 168.4 all-reduce.12
  1086.5 68.6 reduce-scatter.25
  1159.1 68.8 reduce-scatter.29
  1231.9 68.8 reduce-scatter.27
  1304.7 68.8 reduce-scatter.35
where the time goes:
time: 1390 us; the launch traced here: 1380 us
  waiting for transfers between devices  690 us (50%)
  blocking collectives  179 us (13%)
  other arithmetic  133 us (10%)
  local copies, waits for them, and re-layouts  119 us (9%)
  starting transfers between devices  117 us (8%)
  matrix products  112 us (8%)
  between operations  29.6 us (2%)
    unnamed x24, waiting for transfers between devices  294 us
    ppermute x56, starting transfers between devices, shifted(): lax.ppermute(value, axis, [(source, source + steps) for source in range(i...  116 us
    reduce_scatter x1, waiting for transfers between devices, body(): lax.psum_scatter(sum_downw, 'dp', scatter_dimension=1, tiled=True)  72.8 us
    reduce_scatter x1, waiting for transfers between devices, body(): lax.psum_scatter(sum_upw, 'dp', scatter_dimension=0, tiled=True)  72.8 us
    reduce_scatter x1, waiting for transfers between devices, body(): lax.psum_scatter(sum_qkv, 'dp', scatter_dimension=0, tiled=True)  70.6 us
    unnamed x508, local copies, waits for them, and re-layouts  57.6 us
    unnamed x2, blocking collectives  40.6 us
    psum x1, waiting for transfers between devices, body(): lax.psum(outer_cols(grad_pre, upw_back).astype(jnp.bfloat16), 'mp')  39.4 us
  transfers between devices with their start and end apart: 74, of which 27 were waited for; matrix products, arithmetic and copies ran while one was open for 19% of the time, Pallas kernels for 0%

commit v1 on v0

--- a/solution.py
+++ b/solution.py
@@ -1,6 +1,8 @@
 import jax
 import jax.numpy as jnp
 from jax import lax
+from jax.experimental import pallas as pl
+from jax.experimental.pallas import tpu as pltpu
 from jax.sharding import PartitionSpec as P
 
 HEAD_DIM = 64
@@ -93,7 +95,7 @@
     return ancestors
 
 
-def body(
+def generic_body(
     tokens,
     cotangent,
     qkv_weight,
@@ -398,7 +400,519 @@
     return (mixed, tokens_grad) + tuple(totals)
 
 
+RING = 8
+BF = jnp.bfloat16
+F32 = jnp.float32
+
+
+def ring_dp(place):
+    high = place // 4
+    return high * (2 * (7 - place) + 1) + (1 - high) * (2 * place)
+
+
+def ring_place(index):
+    y_at = index % 2
+    z_at = index // 2
+    return y_at * (7 - z_at) + (1 - y_at) * z_at
+
+
+def ring_at(place, steps):
+    return ring_dp((place + steps + 2 * RING) % RING)
+
+
+def ring_barrier(right, left):
+    barrier = pltpu.get_barrier_semaphore()
+    for other in (right, left):
+        pl.semaphore_signal(
+            barrier, inc=1, device_id={"dp": other}, device_id_type=pl.DeviceIdType.MESH
+        )
+    pl.semaphore_wait(barrier, 2)
+
+
+def half_rows(ref, direction):
+    half = ref.shape[-2] // 2
+    return ref.at[pl.ds(direction * half, half)]
+
+
+def gather_kernel(count, *refs):
+    ins, outs = refs[:count], refs[count : 2 * count]
+    send_sem, recv_sem, own_sem = refs[2 * count :]
+    own = lax.axis_index("dp")
+    place = ring_place(own)
+    sides = (ring_at(place, 1), ring_at(place, -1))
+    ring_barrier(*sides)
+
+    def copy(at, direction, step):
+        origin = ring_at(place, (1 - step) * (1 - 2 * direction))
+        source = ins[at] if step == 1 else outs[at].at[origin]
+        target = outs[at].at[origin]
+        if step == 4:
+            source, target = half_rows(source, direction), half_rows(target, direction)
+        return pltpu.make_async_remote_copy(
+            src_ref=source,
+            dst_ref=target,
+            send_sem=send_sem.at[at, direction, step - 1],
+            recv_sem=recv_sem.at[at, direction, step - 1],
+            device_id={"dp": sides[direction]},
+            device_id_type=pl.DeviceIdType.MESH,
+        )
+
+    mine = [
+        pltpu.make_async_copy(ins[at], outs[at].at[own], own_sem.at[at]) for at in range(count)
+    ]
+    for at in range(count):
+        for direction in (0, 1):
+            copy(at, direction, 1).start()
+        mine[at].start()
+    for step in range(2, 5):
+        for at in range(count):
+            for direction in (0, 1):
+                copy(at, direction, step - 1).wait_recv()
+                copy(at, direction, step).start()
+    for at in range(count):
+        for direction in (0, 1):
+            copy(at, direction, 4).wait_recv()
+        mine[at].wait()
+    for at in range(count):
+        for direction in (0, 1):
+            for step in range(1, 5):
+                copy(at, direction, step).wait_send()
+
+
+def ring_gather(*arrays):
+    count = len(arrays)
+    return pl.pallas_call(
+        lambda *refs: gather_kernel(count, *refs),
+        out_shape=[jax.ShapeDtypeStruct((RING,) + a.shape, a.dtype) for a in arrays],
+        in_specs=[pl.BlockSpec(memory_space=pltpu.VMEM)] * count,
+        out_specs=[pl.BlockSpec(memory_space=pltpu.VMEM)] * count,
+        scratch_shapes=[
+            pltpu.SemaphoreType.DMA((count, 2, 4)),
+            pltpu.SemaphoreType.DMA((count, 2, 4)),
+            pltpu.SemaphoreType.DMA((count,)),
+        ],
+        compiler_params=pltpu.CompilerParams(collective_id=0, has_side_effects=True),
+        name="ring_gather",
+    )(*arrays)
+
+
+def scatter_kernel(count, *refs):
+    ins, outs = refs[:count], refs[count : 2 * count]
+    bufs = refs[2 * count : 3 * count]
+    send_sem, recv_sem = refs[3 * count :]
+    own = lax.axis_index("dp")
+    place = ring_place(own)
+    sides = (ring_at(place, 1), ring_at(place, -1))
+    ring_barrier(*sides)
+
+    def copy(at, direction, step):
+        source = bufs[at].at[direction, step - 1]
+        target = bufs[at].at[direction, step]
+        if step == 1:
+            source, target = half_rows(source, direction), half_rows(target, direction)
+        return pltpu.make_async_remote_copy(
+            src_ref=source,
+            dst_ref=target,
+            send_sem=send_sem.at[at, direction, step - 1],
+            recv_sem=recv_sem.at[at, direction, step - 1],
+            device_id={"dp": sides[direction]},
+            device_id_type=pl.DeviceIdType.MESH,
+        )
+
+    def term(at, direction, step):
+        aim = ring_at(place, (5 - step) * (1 - 2 * direction))
+        return ins[at].at[aim]
+
+    for at in range(count):
+        for direction in (0, 1):
+            half = outs[at].shape[0] // 2
+            part = pl.ds(direction * half, half)
+            bufs[at][direction, 0, part] = term(at, direction, 1)[part].astype(bufs[at].dtype)
+            copy(at, direction, 1).start()
+    for step in range(2, 5):
+        for at in range(count):
+            for direction in (0, 1):
+                buf = bufs[at]
+                copy(at, direction, step - 1).wait_recv()
+                if step == 2:
+                    half = outs[at].shape[0] // 2
+                    part = pl.ds(direction * half, half)
+                    rest = pl.ds((1 - direction) * half, half)
+                    buf[direction, 1, part] = (
+                        buf[direction, 1, part].astype(F32) + term(at, direction, 2)[part]
+                    ).astype(buf.dtype)
+                    buf[direction, 1, rest] = term(at, direction, 2)[rest].astype(buf.dtype)
+                else:
+                    buf[direction, step - 1] = (
+                        buf[direction, step - 1].astype(F32) + term(at, direction, step)[...]
+                    ).astype(buf.dtype)
+                copy(at, direction, step).start()
+    for at in range(count):
+        for direction in (0, 1):
+            copy(at, direction, 4).wait_recv()
+        outs[at][...] = (
+            ins[at][own] + bufs[at][0, 4].astype(F32) + bufs[at][1, 4].astype(F32)
+        )
+    for at in range(count):
+        for direction in (0, 1):
+            for step in range(1, 5):
+                copy(at, direction, step).wait_send()
+
+
+def ring_scatter(arrays, kinds):
+    count = len(arrays)
+    return pl.pallas_call(
+        lambda *refs: scatter_kernel(count, *refs),
+        out_shape=[jax.ShapeDtypeStruct(a.shape[1:], F32) for a in arrays],
+        in_specs=[pl.BlockSpec(memory_space=pltpu.VMEM)] * count,
+        out_specs=[pl.BlockSpec(memory_space=pltpu.VMEM)] * count,
+        scratch_shapes=[
+            pltpu.VMEM((2, 5) + a.shape[1:], kind) for a, kind in zip(arrays, kinds)
+        ]
+        + [pltpu.SemaphoreType.DMA((count, 2, 4)), pltpu.SemaphoreType.DMA((count, 2, 4))],
+        compiler_params=pltpu.CompilerParams(
+            collective_id=1, has_side_effects=True, vmem_limit_bytes=60 * 1024 * 1024
+        ),
+        name="ring_scatter",
+    )(*arrays)
+
+
+def gather_weights(
+    qkv_weight, head_bias, out_weight, up_weight, up_bias, down_weight, mem_qk, mem_value,
+    norm_gain, shift_bias,
+):
+    rows, parts, cols = qkv_weight.shape
+    small = jnp.concatenate(
+        [
+            jnp.pad(head_bias[:, 0], ((0, 0), (0, rows - head_bias.shape[2]))),
+            up_bias,
+            norm_gain,
+            shift_bias,
+        ],
+        0,
+    )
+    small = jnp.pad(small, ((0, 32 - small.shape[0]), (0, 128 - rows)))
+    memk, memv, memq, qkv, outw, upw, downw, small = ring_gather(
+        mem_qk[1], mem_value, mem_qk[0], qkv_weight.reshape(rows, parts * cols), out_weight.T,
+        up_weight, down_weight.T, small,
+    )
+    width = RING * rows
+    rows_of = small[:, :9, :rows].transpose(1, 0, 2)
+    flat = rows_of.reshape(9, width)
+    hbias = rows_of[:2, :, : head_bias.shape[2]].reshape(2, 1, -1)
+    return (
+        qkv.reshape(width, parts, cols),
+        hbias,
+        outw.reshape(width, -1).T,
+        upw.reshape(width, -1),
+        flat[2:3],
+        downw.reshape(width, -1).T,
+        jnp.stack([memq.reshape(width, width), memk.reshape(width, width)]),
+        memv.reshape(width, width),
+        flat[3:5],
+        flat[5:9],
+    )
+
+
+def scatter_grads(qkv, hbias, outw, upw, ubias, downw, memqk, memv, gains, shifts):
+    width, parts, cols = qkv.shape
+    rows = width // RING
+    heads = cols // RING
+    small = jnp.concatenate(
+        [
+            jnp.pad(hbias.reshape(2, RING, heads), ((0, 0), (0, 0), (0, rows - heads))),
+            ubias.reshape(1, RING, rows),
+            gains.reshape(2, RING, rows),
+            shifts.reshape(4, RING, rows),
+        ],
+        0,
+    ).transpose(1, 0, 2)
+    small = jnp.pad(small, ((0, 0), (0, 16 - 9), (0, 128 - rows)))
+
+    def cut(value):
+        return value.reshape(RING, rows, -1)
+
+    down, up, out, qkv, memq, memk, memv, small = ring_scatter(
+        [
+            cut(downw.T), cut(upw), cut(outw.T), cut(qkv.reshape(width, -1)), cut(memqk[0]),
+            cut(memqk[1]), cut(memv), small,
+        ],
+        [BF] * 7 + [F32],
+    )
+    return (
+        qkv.reshape(rows, parts, cols),
+        small[:2, :heads].reshape(2, 1, heads),
+        out.T,
+        up,
+        small[2:3, :rows],
+        down.T,
+        jnp.stack([memq, memk]),
+        memv,
+        small[3:5, :rows],
+        small[5:9, :rows],
+    )
+
+
+def ring_body(
+    tokens,
+    cotangent,
+    qkv_weight,
+    head_bias,
+    out_weight,
+    up_weight,
+    up_bias,
+    down_weight,
+    mem_qk,
+    mem_value,
+    norm_gain,
+    shift_bias,
+    parents,
+):
+    own_index = lax.axis_index("dp")
+    own_slot = own_index % TREE
+    seg_len = tokens.shape[1]
+    model_width = mem_value.shape[1]
+    local_cols = qkv_weight.shape[2]
+    heads_local = local_cols // HEAD_DIM
+    group_rows = TREE * MEM
+    score_scale = HEAD_DIM ** (-0.5)
+    share_rows = seg_len // lax.axis_size("mp")
+    share_start = lax.axis_index("mp") * share_rows
+    rows_index = jnp.arange(seg_len)
+    causal = rows_index[:, None] >= rows_index[None, :]
+    totals = None
+    (qkv_full, hbias_full, outw_full, upw_full, ubias_full, downw_full, memqk_full, memv_full,
+     gains_full, shifts_full) = gather_weights(
+        qkv_weight, head_bias, out_weight, up_weight, up_bias, down_weight, mem_qk, mem_value,
+        norm_gain, shift_bias)
+    outputs = []
+    input_grads = []
+    for micro_index in range(MICRO):
+        inputs = tokens[micro_index]
+        memory_rows = inputs[seg_len - MEM :]
+        key_raw = jnp.dot(memory_rows, memqk_full[1], preferred_element_type=jnp.float32)
+        value_raw = jnp.dot(memory_rows, memv_full, preferred_element_type=jnp.float32)
+        key_low = key_raw.astype(jnp.bfloat16)
+        value_low = value_raw.astype(jnp.bfloat16)
+        empty_group = jnp.zeros((group_rows, model_width), jnp.bfloat16)
+        group_keys = lax.dynamic_update_slice_in_dim(empty_group, key_low, own_slot * MEM, 0)
+        group_values = lax.dynamic_update_slice_in_dim(empty_group, value_low, own_slot * MEM, 0)
+        for hop_count in range(1, TREE):
+            far_keys, far_values = shifted((key_low, value_low), "dp", hop_count)
+            far_slot = own_slot - hop_count
+            inside = far_slot >= 0
+            place_at = jnp.maximum(far_slot, 0) * MEM
+            group_keys = jnp.where(
+                inside,
+                lax.dynamic_update_slice_in_dim(group_keys, far_keys, place_at, 0),
+                group_keys,
+            )
+            group_values = jnp.where(
+                inside,
+                lax.dynamic_update_slice_in_dim(group_values, far_values, place_at, 0),
+                group_values,
+            )
+        group_keys_f = group_keys.astype(jnp.float32)
+        key_feats = dpfp_rounded(group_keys_f)
+        row_mask = jnp.repeat(path_marks(parents[micro_index], own_index), MEM)
+        query_raw = jnp.dot(inputs, memqk_full[0], preferred_element_type=jnp.float32)
+        query_feats = dpfp_rounded(query_raw)
+        masked_scores = outer_cols(query_feats, key_feats) * row_mask[None, :]
+        read_weights = masked_scores.astype(jnp.bfloat16)
+        denominator = jnp.sum(masked_scores, -1, keepdims=True) + 1.0
+        numerator = jnp.dot(read_weights, group_values, preferred_element_type=jnp.float32)
+        hidden = inputs.astype(jnp.float32) + numerator / denominator
+        attn_in = layer_norm(hidden, gains_full[0], shifts_full[0]).astype(jnp.bfloat16)
+        projected = jnp.einsum("sd,dcf->scf", attn_in, qkv_full, preferred_element_type=jnp.float32)
+        bias_pair = hbias_full.reshape(2, local_cols).astype(jnp.float32)
+        shape_heads = (seg_len, heads_local, HEAD_DIM)
+        queries = (projected[:, 0] + bias_pair[0]).astype(jnp.bfloat16).reshape(shape_heads)
+        key_heads = projected[:, 1].astype(jnp.bfloat16).reshape(shape_heads)
+        value_heads = (projected[:, 2] + bias_pair[1]).astype(jnp.bfloat16).reshape(shape_heads)
+        scores = (
+            jnp.einsum("qhd,khd->hqk", queries, key_heads, preferred_element_type=jnp.float32)
+            * score_scale
+        )
+        scores = jnp.where(causal[None], scores, -jnp.inf)
+        row_max = jnp.max(scores, -1, keepdims=True)
+        exponents = jnp.exp(scores - row_max)
+        row_total = jnp.sum(exponents, -1, keepdims=True)
+        log_total = row_max + jnp.log(row_total)
+        prob_low = (exponents / row_total).astype(jnp.bfloat16)
+        attended = jnp.einsum(
+            "hqk,khd->qhd", prob_low, value_heads, preferred_element_type=jnp.float32
+        )
+        attended = attended.astype(jnp.bfloat16).reshape(seg_len, local_cols)
+        attn_out = (
+            lax.psum(
+                jnp.dot(attended, outw_full, preferred_element_type=jnp.float32).astype(
+                    jnp.bfloat16
+                ),
+                "mp",
+            ).astype(jnp.float32)
+            + shifts_full[2]
+        )
+        middle = hidden + attn_out
+        normed_two = layer_norm(middle, gains_full[1], shifts_full[1]).astype(jnp.bfloat16)
+        pre_act = jnp.dot(normed_two, upw_full, preferred_element_type=jnp.float32) + ubias_full[0]
+        activated = gelu_tanh(pre_act).astype(jnp.bfloat16)
+        mlp_share = lax.psum_scatter(
+            jnp.dot(activated, downw_full, preferred_element_type=jnp.float32).astype(jnp.bfloat16),
+            "mp",
+            scatter_dimension=0,
+            tiled=True,
+        ).astype(jnp.float32)
+        middle_share = lax.dynamic_slice_in_dim(middle, share_start, share_rows, 0)
+        outputs.append((middle_share + mlp_share + shifts_full[3]).astype(jnp.bfloat16))
+        qkv_back, outw_back, upw_back, downw_back = qkv_full, outw_full, upw_full, downw_full
+        memqk_back, memv_back, gains_back, shifts_back = memqk_full, memv_full, gains_full, shifts_full
+        grad_out = cotangent[micro_index]
+        grad_out_f = grad_out.astype(jnp.float32)
+        grad_downw = inner_rows(activated, grad_out)
+        grad_act = outer_cols(grad_out, downw_back)
+        gelu_value, gelu_back = jax.vjp(gelu_tanh, pre_act)
+        grad_pre = gelu_back(grad_act)[0].astype(jnp.bfloat16)
+        grad_ubias = jnp.sum(grad_pre.astype(jnp.float32), 0)[None, :]
+        grad_upw = inner_rows(normed_two, grad_pre)
+        grad_norm_two = lax.psum(outer_cols(grad_pre, upw_back).astype(jnp.bfloat16), "mp").astype(
+            jnp.float32
+        )
+        norm_value, norm_two_back = jax.vjp(layer_norm, middle, gains_back[1], shifts_back[1])
+        grad_mid_norm, gain_two, shift_two = norm_two_back(grad_norm_two)
+        grad_middle = grad_out_f + grad_mid_norm
+        grad_attn = grad_middle.astype(jnp.bfloat16)
+        grad_outw = inner_rows(attended, grad_attn)
+        grad_attended = outer_cols(grad_attn, outw_back).astype(jnp.bfloat16).reshape(shape_heads)
+        scores_again = (
+            jnp.einsum("qhd,khd->hqk", queries, key_heads, preferred_element_type=jnp.float32)
+            * score_scale
+        )
+        scores_again = jnp.where(causal[None], scores_again, -jnp.inf)
+        prob_full = jnp.exp(scores_again - log_total)
+        prob_again = prob_full.astype(jnp.bfloat16)
+        grad_values = jnp.einsum(
+            "hqk,qhd->khd", prob_again, grad_attended, preferred_element_type=jnp.float32
+        )
+        grad_probs = jnp.einsum(
+            "qhd,khd->hqk", grad_attended, value_heads, preferred_element_type=jnp.float32
+        )
+        row_delta = jnp.sum(prob_full * grad_probs, -1, keepdims=True)
+        grad_scores = (prob_full * (grad_probs - row_delta)).astype(jnp.bfloat16)
+        grad_queries = (
+            jnp.einsum("hqk,khd->qhd", grad_scores, key_heads, preferred_element_type=jnp.float32)
+            * score_scale
+        )
+        grad_keys = (
+            jnp.einsum("hqk,qhd->khd", grad_scores, queries, preferred_element_type=jnp.float32)
+            * score_scale
+        )
+        grad_proj = (
+            jnp.stack([grad_queries, grad_keys, grad_values], 1)
+            .reshape(seg_len, 3, local_cols)
+            .astype(jnp.bfloat16)
+        )
+        grad_proj_f = grad_proj.astype(jnp.float32)
+        grad_hbias = jnp.stack(
+            [jnp.sum(grad_proj_f[:, 0], 0), jnp.sum(grad_proj_f[:, 2], 0)]
+        ).reshape(2, 1, local_cols)
+        grad_qkv = jnp.einsum("sd,scf->dcf", attn_in, grad_proj, preferred_element_type=jnp.float32)
+        grad_norm_one = lax.psum(
+            jnp.einsum(
+                "scf,dcf->sd", grad_proj, qkv_back, preferred_element_type=jnp.float32
+            ).astype(jnp.bfloat16),
+            "mp",
+        ).astype(jnp.float32)
+        norm_value_one, norm_one_back = jax.vjp(layer_norm, hidden, gains_back[0], shifts_back[0])
+        grad_hid_norm, gain_one, shift_one = norm_one_back(grad_norm_one)
+        grad_hidden = grad_middle + grad_hid_norm
+        ratio_value, divide_back = jax.vjp(divide_rows, numerator, denominator)
+        grad_numerator, grad_denominator = divide_back(grad_hidden)
+        grad_numerator_b = grad_numerator.astype(jnp.bfloat16)
+        grad_read = outer_cols(grad_numerator_b, group_values)
+        grad_values_group = inner_rows(read_weights, grad_numerator_b)
+        grad_assoc = ((grad_read + grad_denominator) * row_mask[None, :]).astype(jnp.bfloat16)
+        grad_query_feats = jnp.dot(grad_assoc, key_feats, preferred_element_type=jnp.float32)
+        grad_key_feats = inner_rows(grad_assoc, query_feats)
+        grad_query = dpfp_backward(query_raw, grad_query_feats).astype(jnp.bfloat16)
+        grad_keys_group = dpfp_backward(group_keys_f, grad_key_feats)
+        own_keys = lax.dynamic_slice_in_dim(grad_keys_group, own_slot * MEM, MEM, 0)
+        own_values = lax.dynamic_slice_in_dim(grad_values_group, own_slot * MEM, MEM, 0)
+        for hop_count in range(1, TREE):
+            far_slot = own_slot - hop_count
+            inside = far_slot >= 0
+            take_at = jnp.maximum(far_slot, 0) * MEM
+            send_keys = jnp.where(
+                inside, lax.dynamic_slice_in_dim(grad_keys_group, take_at, MEM, 0), 0.0
+            )
+            send_values = jnp.where(
+                inside, lax.dynamic_slice_in_dim(grad_values_group, take_at, MEM, 0), 0.0
+            )
+            back_keys, back_values = (
+                shifted(send_keys.astype(jnp.bfloat16), "dp", -hop_count).astype(send_keys.dtype),
+                shifted(send_values.astype(jnp.bfloat16), "dp", -hop_count).astype(
+                    send_values.dtype
+                ),
+            )
+            arrive = own_slot + hop_count < TREE
+            own_keys = own_keys + jnp.where(arrive, back_keys, 0.0)
+            own_values = own_values + jnp.where(arrive, back_values, 0.0)
+        own_keys_b = own_keys.astype(jnp.bfloat16)
+        own_values_b = own_values.astype(jnp.bfloat16)
+        grad_memqk = jnp.stack(
+            [inner_rows(inputs, grad_query), inner_rows(memory_rows, own_keys_b)]
+        )
+        grad_memv = inner_rows(memory_rows, own_values_b)
+        memory_part = outer_cols(own_keys_b, memqk_back[1]) + outer_cols(own_values_b, memv_back)
+        padding = jnp.zeros((seg_len - MEM, model_width), jnp.float32)
+        grad_inputs = (
+            grad_hidden
+            + outer_cols(grad_query, memqk_back[0])
+            + jnp.concatenate([padding, memory_part], 0)
+        )
+        input_grads.append(grad_inputs.astype(jnp.bfloat16))
+        grad_gains = jnp.stack([gain_one, gain_two])
+        grad_shifts = jnp.stack(
+            [shift_one, shift_two, jnp.sum(grad_middle, 0), jnp.sum(grad_out_f, 0)]
+        )
+        shares = (
+            grad_qkv,
+            grad_hbias,
+            grad_outw,
+            grad_upw,
+            grad_ubias,
+            grad_downw,
+            grad_memqk,
+            grad_memv,
+            grad_gains,
+            grad_shifts,
+        )
+        totals = (
+            shares
+            if totals is None
+            else tuple((older + newer for older, newer in zip(totals, shares)))
+        )
+    (
+        sum_qkv,
+        sum_hbias,
+        sum_outw,
+        sum_upw,
+        sum_ubias,
+        sum_downw,
+        sum_memqk,
+        sum_memv,
+        sum_gains,
+        sum_shifts,
+    ) = totals
+    totals = scatter_grads(
+        sum_qkv, sum_hbias, sum_outw, sum_upw, sum_ubias, sum_downw, sum_memqk, sum_memv,
+        sum_gains, sum_shifts)
+    mixed = jnp.stack(outputs)
+    tokens_grad = jnp.stack(input_grads)
+    return (mixed, tokens_grad) + tuple(totals)
+
+
 def solution(mesh):
+    body = ring_body if mesh.shape["dp"] == RING else generic_body
     return jax.shard_map(
         body,
         mesh=mesh,

time: 1390 us -> 796 us (0.57)
  waiting for transfers between devices: 690 us -> 111 us
  blocking collectives: 179 us -> 0 us
  Pallas kernels: 0 us -> 157 us
  starting transfers between devices: 117 us -> 137 us
  matrix products: 112 us -> 96.1 us
    unnamed x24 -> x5, waiting for transfers between devices: 294 us -> 0.08 us
    reduce_scatter x5 -> x2, waiting for transfers between devices: 216 us -> 0.04 us  [ring_body(): lax.psum_scatter(jnp.dot(activated, downw_full, preferred_element_type=jn...]
    pallas_call x0 -> x2, Pallas kernels: none -> 157 us  [the longest x1 79.4 us: ring_gather(): pl.pallas_call(lambda *refs: gather_kernel(count, *refs), out_shape=[jax....]
    all_gather x5 -> x0, blocking collectives: 139 us -> none  [the longest x1 34.7 us: body(): lax.all_gather(qkv_weight, 'dp', axis=0, tiled=True)]
    all_gather x4 -> x0, waiting for transfers between devices: 75.6 us -> none  [the longest x1 38 us: body(): lax.all_gather(down_weight, 'dp', axis=1, tiled=True)]
    unnamed x2 -> x0, blocking collectives: 40.6 us -> none
    unnamed x508 -> x627, local copies, waits for them, and re-layouts: 57.6 us -> 37 us
    ppermute x56, starting transfers between devices: 116 us -> 136 us  [shifted(): lax.ppermute(value, axis, [(source, source + steps) for source in range(i...]
  transfers between devices with their start and end apart: 74 -> 61, of which waited for: 27 -> 23; matrix products, arithmetic and copies ran while one was open for 19% -> 30% of each run, Pallas kernels for 0% -> 0%
where the time goes in v1:
time: 796 us; the launch traced here: 784 us
  Pallas kernels  157 us (20%)
  starting transfers between devices  137 us (17%)
  other arithmetic  134 us (17%)
  local copies, waits for them, and re-layouts  122 us (15%)
  waiting for transfers between devices  111 us (14%)
  matrix products  96.1 us (12%)
  between operations  27.5 us (3%)
    ppermute x56, starting transfers between devices, shifted(): lax.ppermute(value, axis, [(source, source + steps) for source in range(i...  136 us
    pallas_call x1, Pallas kernels, ring_gather(): pl.pallas_call(lambda *refs: gather_kernel(count, *refs), out_shape=[jax....  79.4 us
    pallas_call x1, Pallas kernels, ring_scatter(): pl.pallas_call(lambda *refs: scatter_kernel(count, *refs), out_shape=[jax...  77.3 us
    psum x1, waiting for transfers between devices, ring_body(): lax.psum(jnp.dot(attended, outw_full, preferred_element_type=jnp.float32)...  41.6 us
    unnamed x627, local copies, waits for them, and re-layouts  37 us
    psum x1, waiting for transfers between devices, ring_body(): lax.psum(outer_cols(grad_pre, upw_back).astype(jnp.bfloat16), 'mp')  35.3 us
    ppermute x56, waiting for transfers between devices, shifted(): lax.ppermute(value, axis, [(source, source + steps) for source in range(i...  33.7 us
    slice x24, local copies, waits for them, and re-layouts, dpfp_backward(): jnp.roll(piece * rectified, -roll_by, -1)  29.6 us
  transfers between devices with their start and end apart: 61, of which 23 were waited for; matrix products, arithmetic and copies ran while one was open for 30% of the time, Pallas kernels for 0%

profile of v1, /device:TPU:0, one launch (start us, length us, event | category | flops | bytes accessed | tf_op | source)
XLA Modules:
  0.0 784.1 jit_solution(2476474895619445843)
XLA Ops:
  13.8 79.4 %ring_gather.1 = (bf16[8,96,768]{2,1,0:T(8,128)(2,1)}, bf16[8,96,768]{2,1,0:T(8,128)(2,1)}, bf16[8,96,768]{2,1,0:T(8,128)(2,1)}, bf16[8,96,576]{2,1,0:T(8,128)(2...) custom-call(bf16[96,768]{1,0:T(8,128)(2,1)} %get-tuple-element.204.r, ...), custom_call_target="tpu_custom_call" | custom-call | tf_op jit(solution)/shard_map/ring_gather/pallas_call | solution.py:484
  95.6 5.0 collective-permute-start.26
  107.2 4.0 collective-permute-start.14
  152.3 7.0 multiply_convert_fusion.4
  178.3 4.2 collective-permute-start.1
  189.6 5.3 collective-permute-start.2
  196.6 7.0 collective-permute-start.17
  205.3 5.1 collective-permute-start.3
  216.2 6.0 collective-permute-start.4
  223.9 7.8 collective-permute-start.20
  236.0 4.7 collective-permute-start.6
  253.8 5.0 collective-permute-start.22
  260.5 6.3 collective-permute-start.27
  277.6 4.9 collective-permute-start.8
  311.5 41.6 %all-reduce.17.cloned.1.call-done = (bf16[512,768]{1,0:T(8,128)(2,1)}, bf16[512,768]{1,0:T(8,128)(2,1)}) async-done(((bf16[512,768]{1,0:T(8,128)(2,1)}, bf16[512,768]{1,0:T(8,128)(2,1)}), (bf16[512,768]{1,0:T(8,128)(2,1)}, bf16[512,768]{1,0:T(8,128)(2,1)})) %all-reduce.17.cloned.1.call-update) | async-done | bytes 1572880 | tf_op jit(solution)/shard_map/psum | solution.py:747
  378.2 35.3 %all-reduce.15.cloned.1.call-done = (bf16[512,768]{1,0:T(8,128)(2,1)}, bf16[512,768]{1,0:T(8,128)(2,1)}) async-done(((bf16[512,768]{1,0:T(8,128)(2,1)}, bf16[512,768]{1,0:T(8,128)(2,1)}), (bf16[512,768]{1,0:T(8,128)(2,1)}, bf16[512,768]{1,0:T(8,128)(2,1)})) %all-reduce.15.cloned.1.call-update) | async-done | bytes 1572880 | tf_op jit(solution)/shard_map/psum | solution.py:777
  530.8 8.8 %slice_multiply_fusion = (f32[512,1536]{0,1:T(8,128)}, f32[512,1536]{0,1:T(8,128)}, f32[512,1536]{0,1:T(8,128)}) fusion(f32[512,4608]{0,1:T(8,128)S(1)} %fusion.127, f32[512,768]{0,1:T(8,128)} %copy-done.8, f32[512,768]{0,1:T(8,128)} %copy-done.11), kind=kLoop, calls=%fused_computation.57 | loop fusion | flops 3145728 | bytes 22020096 | tf_op jit(solution)/shard_map/mul | solution.py:57
  540.9 4.1 slice.598
  551.6 9.0 %slice_multiply_fusion.3 = (f32[512,1536]{0,1:T(8,128)}, f32[512,1536]{0,1:T(8,128)}, f32[512,1536]{0,1:T(8,128)}) fusion(f32[512,4608]{0,1:T(8,128)S(1)} %fusion.128, f32[512,768]{0,1:T(8,128)} %copy-done.7, f32[512,768]{0,1:T(8,128)} %copy-done.9), kind=kLoop, calls=%fused_computation.60 | loop fusion | flops 3145728 | bytes 22020096 | tf_op jit(solution)/shard_map/mul | solution.py:57
  588.7 4.1 fusion.107
  594.9 8.1 %fusion.13 = f32[512,1536]{0,1:T(8,128)S(1)} fusion(f32[512,1]{0,1:T(1,128)S(1)} %copy-done.288, f32[512,1535]{0,1:T(8,128)} %slice.598, f32[512,2]{0,1:T(2,128)S(1)} %slice.602, f32[512,1534]{0,1:T(8,128)} %slice.601, f32[512,3]{0,1:T(4,128)S(1)} %slice.605, f32[512,1533]{0,1:T(8,128)} %slice.604, f32[512,4608]{0,1:T(8,128)} %copy-done.1, ...), kind=kLoop, calls=%fused_computation.38 | loop fusion | flops 11010048 | bytes 31457280 | tf_op jit(solution)/shard_map/add | solution.py:55
  614.4 6.3 fusion.9
  655.4 3.7 collective-permute-done.34
  684.7 77.3 %ring_scatter.1 = (f32[96,768]{1,0:T(8,128)}, f32[96,768]{1,0:T(8,128)}, f32[96,192]{1,0:T(8,128)}, f32[96,576]{1,0:T(8,128)}, f32[96,768]{1,0:T(8,128)}, /*inde...) custom-call(f32[8,96,768]{2,1,0:T(8,128)} %bitcast.322, f32[8,96,768]{2,1,0:T(8,128)} %bitcast.324, ...), custom_call_target="tpu_custom_call" | custom-call | tf_op jit(solution)/shard_map/ring_scatter/pallas_call | solution.py:564
  (1029 shorter events, 406.6 us)
Async XLA Ops:
  7.2 345.9 %all-reduce.17.cloned.1.call-start = ((), (), s32[]{:S(2)}) async-start(), calls=%async_computation.6 | async-start | bytes 3145728 | tf_op jit(solution)/shard_map/psum | solution.py:747
  95.6 175.7 %collective-permute-start.26 = (bf16[16,768]{1,0:T(8,128)(2,1)}, bf16[16,768]{1,0:T(8,128)(2,1)}, u32[]{:S(2)}, u32[]{:S(2)}) collective-permute-start(bf16[16,768]{1,0:T(8,128)(2,1)} %get-tuple-element.226), channel_id=1, source_target_pairs={{0,24},{4,28},{1,25},{5,29},{2,26},{6,30},{3,27},{7,31}} | collective-permute-start | bytes 73736 | tf_op jit(solution)/shard_map/ppermute | solution.py:20
  100.6 169.4 %collective-permute-start.25 = (bf16[16,768]{1,0:T(8,128)(2,1)}, bf16[16,768]{1,0:T(8,128)(2,1)}, u32[]{:S(2)}, u32[]{:S(2)}) collective-permute-start(bf16[16,768]{1,0:T(8,128)(2,1)} %get-tuple-element.226), channel_id=1, source_target_pairs={{0,20},{4,24},{8,28},{1,21},{5,25},{9,29},{2,22},{6,26},{10,30},{3... | collective-permute-start | bytes 73736 | tf_op jit(solution)/shard_map/ppermute | solution.py:20
  102.5 166.2 %collective-permute-start.24 = (bf16[16,768]{1,0:T(8,128)(2,1)}, bf16[16,768]{1,0:T(8,128)(2,1)}, u32[]{:S(2)}, u32[]{:S(2)}) collective-permute-start(bf16[16,768]{1,0:T(8,128)(2,1)} %get-tuple-element.226), channel_id=1, source_target_pairs={{0,16},{4,20},{8,24},{12,28},{1,17},{5,21},{9,25},{13,29},{2,18},{... | collective-permute-start | bytes 73736 | tf_op jit(solution)/shard_map/ppermute | solution.py:20
  105.3 126.4 %collective-permute-start.19 = (bf16[16,768]{1,0:T(8,128)(2,1)}, bf16[16,768]{1,0:T(8,128)(2,1)}, u32[]{:S(2)}, u32[]{:S(2)}) collective-permute-start(bf16[16,768]{1,0:T(8,128)(2,1)} %get-tuple-element.228), channel_id=1, source_target_pairs={{0,24},{4,28},{1,25},{5,29},{2,26},{6,30},{3,27},{7,31}} | collective-permute-start | bytes 73736 | tf_op jit(solution)/shard_map/ppermute | solution.py:20
  107.2 62.5 %collective-permute-start.14 = (bf16[16,768]{1,0:T(8,128)(2,1)}, bf16[16,768]{1,0:T(8,128)(2,1)}, u32[]{:S(2)}, u32[]{:S(2)}) collective-permute-start(bf16[16,768]{1,0:T(8,128)(2,1)} %get-tuple-element.228), channel_id=1, source_target_pairs={{0,4},{4,8},{8,12},{12,16},{16,20},{20,24},{24,28},{1,5},{5,9},{9,... | collective-permute-start | bytes 73736 | tf_op jit(solution)/shard_map/ppermute | solution.py:20
  223.9 16.9 %collective-permute-start.20 = (bf16[16,768]{1,0:T(8,128)(2,1)}, bf16[16,768]{1,0:T(8,128)(2,1)S(1)}, u32[]{:S(2)}, u32[]{:S(2)}) collective-permute-start(bf16[16,768]{1,0:T(8,128)(2,1)} %get-tuple-element.228), channel_id=1, source_target_pairs={{0,28},{1,29},{2,30},{3,31}} | collective-permute-start | bytes 73736 | tf_op jit(solution)/shard_map/ppermute | solution.py:20
  240.8 26.0 %collective-permute-start.23 = (bf16[16,768]{1,0:T(8,128)(2,1)}, bf16[16,768]{1,0:T(8,128)(2,1)S(1)}, u32[]{:S(2)}, u32[]{:S(2)}) collective-permute-start(bf16[16,768]{1,0:T(8,128)(2,1)} %get-tuple-element.226), channel_id=1, source_target_pairs={{0,12},{4,16},{8,20},{12,24},{16,28},{1,13},{5,17},{9,21},{13,25},... | collective-permute-start | bytes 73736 | tf_op jit(solution)/shard_map/ppermute | solution.py:20
  266.8 21.0 %collective-permute-start.12 = (bf16[16,768]{1,0:T(8,128)(2,1)S(1)}, bf16[16,768]{1,0:T(8,128)(2,1)S(1)}, u32[]{:S(2)}, u32[]{:S(2)}) collective-permute-start(bf16[16,768]{1,0:T(8,128)(2,1)S(1)} %copy-done.216), channel_id=1, source_target_pairs={{0,24},{4,28},{1,25},{5,29},{2,26},{6,30},{3,27},{7,31}} | collective-permute-start | bytes 73736 | tf_op jit(solution)/shard_map/ppermute | solution.py:20
  268.7 18.5 %collective-permute-start.11 = (bf16[16,768]{1,0:T(8,128)(2,1)S(1)}, bf16[16,768]{1,0:T(8,128)(2,1)S(1)}, u32[]{:S(2)}, u32[]{:S(2)}) collective-permute-start(bf16[16,768]{1,0:T(8,128)(2,1)S(1)} %copy-done.216), channel_id=1, source_target_pairs={{0,20},{4,24},{8,28},{1,21},{5,25},{9,29},{2,22},{6,26},{10,30},{3... | collective-permute-start | bytes 73736 | tf_op jit(solution)/shard_map/ppermute | solution.py:20
  270.0 17.1 %collective-permute-start.10 = (bf16[16,768]{1,0:T(8,128)(2,1)S(1)}, bf16[16,768]{1,0:T(8,128)(2,1)S(1)}, u32[]{:S(2)}, u32[]{:S(2)}) collective-permute-start(bf16[16,768]{1,0:T(8,128)(2,1)S(1)} %copy-done.216), channel_id=1, source_target_pairs={{0,16},{4,20},{8,24},{12,28},{1,17},{5,21},{9,25},{13,29},{2,18},{... | collective-permute-start | bytes 73736 | tf_op jit(solution)/shard_map/ppermute | solution.py:20
  271.4 15.7 %collective-permute-start.9 = (bf16[16,768]{1,0:T(8,128)(2,1)S(1)}, bf16[16,768]{1,0:T(8,128)(2,1)S(1)}, u32[]{:S(2)}, u32[]{:S(2)}) collective-permute-start(bf16[16,768]{1,0:T(8,128)(2,1)S(1)} %copy-done.216), channel_id=1, source_target_pairs={{0,12},{4,16},{8,20},{12,24},{16,28},{1,13},{5,17},{9,21},{13,25},... | collective-permute-start | bytes 73736 | tf_op jit(solution)/shard_map/ppermute | solution.py:20
  308.4 105.1 %all-reduce.15.cloned.1.call-start = ((), (), s32[]{:S(2)}) async-start(), calls=%async_computation.5 | async-start | bytes 3145728 | tf_op jit(solution)/shard_map/psum | solution.py:777
  370.4 127.0 %all-reduce.13.cloned.1.call-start = ((), (), s32[]{:S(2)}) async-start(), calls=%async_computation.4 | async-start | bytes 3145728 | tf_op jit(solution)/shard_map/psum | solution.py:819
  439.2 185.5 %reduce-scatter.3.cloned.1.call-start = ((), (), s32[]{:S(2)}) async-start(), calls=%async_computation.2 | async-start | bytes 983040 | tf_op jit(solution)/shard_map/reduce_scatter | solution.py:759
  444.1 180.6 %reduce-scatter.5.cloned.1.call-start = ((), (), s32[]{:S(2)}) async-start(), calls=%async_computation.3 | async-start | bytes 983040 | tf_op jit(solution)/shard_map/reduce_scatter | solution.py:759
  582.0 45.3 %collective-permute-start.49 = (bf16[16,768]{1,0:T(8,128)(2,1)}, bf16[16,768]{1,0:T(8,128)(2,1)}, u32[]{:S(2)}, u32[]{:S(2)}) collective-permute-start(bf16[16,768]{1,0:T(8,128)(2,1)} %get-tuple-element.196), channel_id=1, source_target_pairs={{4,0},{8,4},{12,8},{16,12},{20,16},{24,20},{28,24},{5,1},{9,5},{13... | collective-permute-start | bytes 73736 | tf_op jit(solution)/shard_map/ppermute | solution.py:20
  583.3 45.5 %collective-permute-start.55 = (bf16[16,768]{1,0:T(8,128)(2,1)}, bf16[16,768]{1,0:T(8,128)(2,1)}, u32[]{:S(2)}, u32[]{:S(2)}) collective-permute-start(bf16[16,768]{1,0:T(8,128)(2,1)} %get-tuple-element.197), channel_id=1, source_target_pairs={{28,0},{29,1},{30,2},{31,3}} | collective-permute-start | bytes 73736 | tf_op jit(solution)/shard_map/ppermute | solution.py:20
  584.6 46.2 %collective-permute-start.54 = (bf16[16,768]{1,0:T(8,128)(2,1)}, bf16[16,768]{1,0:T(8,128)(2,1)}, u32[]{:S(2)}, u32[]{:S(2)}) collective-permute-start(bf16[16,768]{1,0:T(8,128)(2,1)} %get-tuple-element.198), channel_id=1, source_target_pairs={{24,0},{28,4},{25,1},{29,5},{26,2},{30,6},{27,3},{31,7}} | collective-permute-start | bytes 73736 | tf_op jit(solution)/shard_map/ppermute | solution.py:20
  585.9 46.2 %collective-permute-start.53 = (bf16[16,768]{1,0:T(8,128)(2,1)}, bf16[16,768]{1,0:T(8,128)(2,1)}, u32[]{:S(2)}, u32[]{:S(2)}) collective-permute-start(bf16[16,768]{1,0:T(8,128)(2,1)} %get-tuple-element.199), channel_id=1, source_target_pairs={{20,0},{24,4},{28,8},{21,1},{25,5},{29,9},{22,2},{26,6},{30,10},{2... | collective-permute-start | bytes 73736 | tf_op jit(solution)/shard_map/ppermute | solution.py:20
  587.2 46.2 %collective-permute-start.52 = (bf16[16,768]{1,0:T(8,128)(2,1)}, bf16[16,768]{1,0:T(8,128)(2,1)}, u32[]{:S(2)}, u32[]{:S(2)}) collective-permute-start(bf16[16,768]{1,0:T(8,128)(2,1)} %get-tuple-element.200), channel_id=1, source_target_pairs={{16,0},{20,4},{24,8},{28,12},{17,1},{21,5},{25,9},{29,13},{18,2},{... | collective-permute-start | bytes 73736 | tf_op jit(solution)/shard_map/ppermute | solution.py:20
  633.4 14.0 %collective-permute-start.40 = (bf16[16,768]{1,0:T(8,128)(2,1)S(1)}, bf16[16,768]{1,0:T(8,128)(2,1)S(1)}, u32[]{:S(2)}, u32[]{:S(2)}) collective-permute-start(bf16[16,768]{1,0:T(8,128)(2,1)S(1)} %copy-done.228), channel_id=1, source_target_pairs={{24,0},{28,4},{25,1},{29,5},{26,2},{30,6},{27,3},{31,7}} | collective-permute-start | bytes 73736 | tf_op jit(solution)/shard_map/ppermute | solution.py:20
  634.8 14.0 %collective-permute-start.39 = (bf16[16,768]{1,0:T(8,128)(2,1)S(1)}, bf16[16,768]{1,0:T(8,128)(2,1)S(1)}, u32[]{:S(2)}, u32[]{:S(2)}) collective-permute-start(bf16[16,768]{1,0:T(8,128)(2,1)S(1)} %copy-done.227), channel_id=1, source_target_pairs={{20,0},{24,4},{28,8},{21,1},{25,5},{29,9},{22,2},{26,6},{30,10},{2... | collective-permute-start | bytes 73736 | tf_op jit(solution)/shard_map/ppermute | solution.py:20
  636.4 13.6 %collective-permute-start.38 = (bf16[16,768]{1,0:T(8,128)(2,1)S(1)}, bf16[16,768]{1,0:T(8,128)(2,1)S(1)}, u32[]{:S(2)}, u32[]{:S(2)}) collective-permute-start(bf16[16,768]{1,0:T(8,128)(2,1)S(1)} %copy-done.226), channel_id=1, source_target_pairs={{16,0},{20,4},{24,8},{28,12},{17,1},{21,5},{25,9},{29,13},{18,2},{... | collective-permute-start | bytes 73736 | tf_op jit(solution)/shard_map/ppermute | solution.py:20
  (347 other events, 2426.7 us)
Sparse Core Ops, SparseCore 0:
  308.5 44.5 all-reduce.16
  370.6 42.9 all-reduce.14
  439.3 42.9 all-reduce.12
  484.6 23.2 reduce-scatter.2
  510.3 23.1 reduce-scatter.4
